TPU v7x, 128 devices: a whole 4x4x4 slice. The times are simulated.
128 devices in a mesh: req: 4 (over x), hid: 32 (over y, z, core).
Axes of the slice: x: 4, y: 4, z: 4, core: 2. Of those that a mesh axis runs over, the one named last changes fastest.
Arguments:
- layer_input: bfloat16 [2048, 7168], P('req', 'hid'), may hold values from -6 to 6
- norm_gain: float32 [7168], replicated, may hold values from 0.1 to 1.9
- qkv_weight: bfloat16 [7168, 21504], P('req', 'hid'), may hold values from -0.09375 to 0.09375
- cache_keys: bfloat16 [4, 4096, 7168], P('req', None, 'hid'), may hold values from -160 to 160
- cache_values: bfloat16 [4, 4096, 7168], P('req', None, 'hid'), may hold values from -8 to 8
- cache_lengths: int32 [4], P('req'), may hold values from 1 to 4096, 10240 in all
- out_weight: bfloat16 [7168, 3584], P('hid'), may hold values from -0.375 to 0.375
- mlp_gain: float32 [3584], replicated, may hold values from 0.1 to 1.9
- gate_weight: bfloat16 [3584, 14336], P(None, 'hid'), may hold values from -0.09375 to 0.09375
- up_weight: bfloat16 [3584, 14336], P(None, 'hid'), may hold values from -0.09375 to 0.09375
- down_weight: bfloat16 [14336, 3584], P('hid'), may hold values from -0.046875 to 0.046875
Outputs:
- block_out: bfloat16 [2048, 3584], P(('req', 'hid'))
All inputs are finite; a program needn't handle non-finite values. No bound on the sum of `cache_lengths` on one device may be relied on, other than what follows from the above.
Results may differ from a plain program's by a relative error of at most 0.02.
Values may be sent and summed in bfloat16 or wider, within the bound.
A program may use at most 128 MiB of HBM per device.

v0:
```python
import jax
import jax.numpy as jnp
from jax import lax
from jax.sharding import PartitionSpec as P

D = 3584
HD = 224
epsilon = 1e-05


def rms_scale(values, gain):
    return values * lax.rsqrt(jnp.mean(values * values, axis=-1, keepdims=True) + epsilon) * gain


def rotate(values, position):
    half = values.shape[-1] // 2
    freq = jnp.exp(-jnp.log(10000.0) * 2.0 * jnp.arange(half, dtype=jnp.float32) / values.shape[-1])
    angle = position.astype(jnp.float32)[:, None, None] * freq[None, None, :]
    cosine = jnp.cos(angle)
    sine = jnp.sin(angle)
    first = values[..., :half]
    second = values[..., half:]
    return jnp.concatenate(
        [first * cosine - second * sine, second * cosine + first * sine], axis=-1
    )


def merge_block(carry, scores, values):
    top, total, accum = carry
    new_top = jnp.maximum(top, jnp.max(scores, axis=2))
    fade = jnp.exp(top - new_top)
    weights = jnp.exp(scores - new_top[:, :, None])
    total = total * fade + jnp.sum(weights, axis=2)
    accum = accum * fade.T[:, :, None] + jnp.einsum(
        "hqk,khd->qhd", weights.astype(jnp.bfloat16), values, preferred_element_type=jnp.float32
    )
    return (new_top, total, accum)


def shards(
    layer_input,
    norm_gain,
    qkv_weight,
    cache_keys,
    cache_values,
    cache_lengths,
    out_weight,
    mlp_gain,
    gate_weight,
    up_weight,
    down_weight,
):
    span = layer_input.shape[0]
    heads_dev = cache_keys.shape[2] // HD
    slots = cache_keys.shape[1]
    scale = HD ** (-0.5)
    whole_input = lax.all_gather(layer_input, "hid", axis=1, tiled=True)
    normed = rms_scale(whole_input.astype(jnp.float32), norm_gain).astype(jnp.bfloat16)
    columns = normed
    projected = jnp.dot(
        columns,
        lax.all_gather(qkv_weight, "req", axis=0, tiled=True),
        preferred_element_type=jnp.float32,
    ).reshape(span, heads_dev, 3, HD)
    length = cache_lengths[0]
    position = length + jnp.arange(span, dtype=jnp.int32)
    query = rotate(projected[:, :, 0], position).astype(jnp.bfloat16)
    fresh_keys = rotate(projected[:, :, 1], position).astype(jnp.bfloat16)
    fresh_values = projected[:, :, 2].astype(jnp.bfloat16)
    cache_k = cache_keys[0].reshape(slots, heads_dev, HD)
    cache_v = cache_values[0].reshape(slots, heads_dev, HD)
    block = min(512, slots)
    block_count = (length + block - 1) // block

    def visit(index, carry):
        keys = lax.dynamic_slice_in_dim(cache_k, index * block, block, 0)
        values = lax.dynamic_slice_in_dim(cache_v, index * block, block, 0)
        scores = jnp.einsum("qhd,khd->hqk", query, keys, preferred_element_type=jnp.float32) * scale
        columns = index * block + jnp.arange(block, dtype=jnp.int32)
        scores = jnp.where(columns[None, None, :] < length, scores, -1e30)
        return merge_block(carry, scores, values)

    start_state = (
        jnp.full((heads_dev, span), -1e30, jnp.float32),
        jnp.zeros((heads_dev, span), jnp.float32),
        jnp.zeros((span, heads_dev, HD), jnp.float32),
    )
    state = lax.fori_loop(0, block_count, visit, start_state)
    fresh_scores = (
        jnp.einsum("qhd,khd->hqk", query, fresh_keys, preferred_element_type=jnp.float32) * scale
    )
    causal = (
        jnp.arange(span, dtype=jnp.int32)[None, :] <= jnp.arange(span, dtype=jnp.int32)[:, None]
    )
    fresh_scores = jnp.where(causal[None, :, :], fresh_scores, -1e30)
    top, total, accum = merge_block(state, fresh_scores, fresh_values)
    heads_out = (accum / total.T[:, :, None]).astype(jnp.bfloat16).reshape(span, heads_dev * HD)
    row_count = span // lax.axis_size("hid")
    row_start = lax.axis_index("hid") * row_count
    attention = lax.psum(
        jnp.dot(heads_out, out_weight, preferred_element_type=jnp.float32).astype(jnp.bfloat16),
        "hid",
    ).astype(jnp.float32)
    mid = (whole_input[:, :D].astype(jnp.float32) + attention).astype(jnp.bfloat16)
    mlp_in = rms_scale(mid.astype(jnp.float32), mlp_gain).astype(jnp.bfloat16)
    gate = jnp.dot(mlp_in, gate_weight, preferred_element_type=jnp.float32)
    upward = jnp.dot(mlp_in, up_weight, preferred_element_type=jnp.float32)
    hidden = (jax.nn.gelu(gate, approximate=True) * upward).astype(jnp.bfloat16)
    mlp_part = lax.psum_scatter(
        jnp.dot(hidden, down_weight, preferred_element_type=jnp.float32).astype(jnp.bfloat16),
        "hid",
        scatter_dimension=0,
        tiled=True,
    ).astype(jnp.float32)
    mid_own = lax.dynamic_slice_in_dim(mid, row_start, row_count, 0)
    return (mid_own.astype(jnp.float32) + mlp_part).astype(jnp.bfloat16)


def solution(mesh):
    placed = (
        P("req", "hid"),
        P(),
        P("req", "hid"),
        P("req", None, "hid"),
        P("req", None, "hid"),
        P("req"),
        P("hid", None),
        P(),
        P(None, "hid"),
        P(None, "hid"),
        P("hid", None),
    )
    return jax.shard_map(
        shards, mesh=mesh, in_specs=placed, out_specs=P(("req", "hid"), None), check_vma=False
    )
```

profile of v0, /device:TPU:0, one launch (start us, length us, event | category | flops | bytes accessed | tf_op | source)
XLA Modules:
  0.0 435.5 jit_solution(8863642717574515305)
XLA Ops:
  6.5 0.0 copy-start
  6.5 0.0 all-gather.3.cloned.1.call-start
  6.5 0.7 all-gather.3.cloned.1.call-update
  7.3 0.0 all-gather.5.cloned.1.call-start
  7.3 0.7 all-gather.5.cloned.1.call-update
  8.0 0.0 all-reduce.2.cloned.1.call-start
  8.7 0.0 copy-start.5
  8.8 54.3 %all-gather.3.cloned.1.call-done = bf16[512,7168]{0,1:T(8,128)(2,1)} async-done(((bf16[512,224]{0,1:T(8,128)(2,1)}), bf16[512,7168]{0,1:T(8,128)(2,1)}) %all-gather.3.cloned.1.call-update) | async-done | bytes 7340048 | tf_op jit(solution)/shard_map/all_gather | solution.py:57
  63.0 4.7 %fusion.13 = f32[512]{0:T(512)S(1)} fusion(bf16[512,7168]{0,1:T(8,128)(2,1)} %all-gather.3.cloned.1.call-done), kind=kLoop, calls=%fused_computation.20 | loop fusion | flops 11009536 | bytes 7342080 | tf_op jit(solution)/shard_map/reduce_sum | solution.py:12
  67.7 89.6 %all-gather.5.cloned.1.call-done = bf16[7168,672]{0,1:T(8,128)(2,1)} async-done(((bf16[1792,672]{0,1:T(8,128)(2,1)}), bf16[7168,672]{0,1:T(8,128)(2,1)}) %all-gather.5.cloned.1.call-update) | async-done | bytes 9633808 | tf_op jit(solution)/shard_map/all_gather | solution.py:62
  157.3 0.0 copy-done.5
  157.3 11.0 %fusion.19 = f32[512,672]{0,1:T(8,128)S(1)} fusion(bf16[7168,672]{0,1:T(8,128)(2,1)} %all-gather.5.cloned.1.call-done, bf16[512,7168]{0,1:T(8,128)(2,1)} %all-gather.3.cloned.1.call-done, f32[7168]{0:T(1024)S(1)} %copy-done.5, f32[512]{0:T(512)S(1)} %add_rsqrt_fusion.1), kind=kOutput, calls=%fused_computation.28 | convolution fusion | flops 4947181568 | bytes 18380800 | tf_op jit(solution)/shard_map/dot_general | solution.py:60
  168.3 0.0 copy-start.3
  168.3 0.1 slice_bitcast_fusion
  168.4 1.7 fusion.78
  170.1 0.0 copy-done.3
  170.1 0.7 pad_maximum_fusion
  170.8 0.9 broadcast_in_dim.26
  171.7 13.9 %while.14 = (s32[]{:T(128)}, f32[1,512]{1,0:T(1,128)S(1)}, f32[1,512]{1,0:T(1,128)S(1)}, f32[512,1,224]{0,2,1:T(8,128)}, s32[]{:T(128)}, /*index=5*/s32[]{:T(128...) while((s32[]{:T(128)}, f32[1,512]{1,0:T(1,128)S(1)}, ...), condition=%wide.region_4.5_spmd, body=%wide.region_1.4_spmd.sunk | while | flops 236947456 | bytes 4785347 | solution.py:88
  171.7 0.7 add_compare_fusion.2
  172.4 1.4 fusion.94
  173.8 0.2 fusion.95
  174.0 2.3 fusion.96
  176.3 0.7 add_compare_fusion.2
  177.0 1.4 fusion.94
  178.4 0.2 fusion.95
  178.6 2.3 fusion.96
  181.0 0.7 add_compare_fusion.2
  181.6 1.4 fusion.94
  183.0 0.2 fusion.95
  183.3 2.3 fusion.96
  185.6 1.3 fusion.81
  186.9 0.0 copy-start.1
  187.0 1.0 copy-done.1
  188.0 0.2 fusion.32
  188.2 5.3 %convolution_convert_fusion = bf16[512,3584]{1,0:T(8,128)(2,1)} fusion(bf16[224,3584]{1,0:T(8,128)(2,1)} %param.19, f32[512,512]{0,1:T(8,128)} %copy-done.1, f32[512]{0:T(512)S(1)} %bitcast.98, f32[512,1,224]{0,2,1:T(8,128)} %get-tuple-element.55, f32[512,1,3,224]{0,3,2,1:T(8,128)} %bitcast.88, f32[512]{0:T(512)S(1)} %bitcast.100, f32[512]{0:T(512)S(1)} %bitcast.101), kind=kOutput, calls=%fused_computation.32 | convolution fusion | flops 942342144 | bytes 7018496 | tf_op jit(solution)/shard_map/dot_general | solution.py:101
  193.5 0.0 all-reduce.2.cloned.1.call-update
  193.5 0.2 reduce-scatter.2.cloned.1.call-start
  193.7 4.1 slice.33
  197.8 5.9 %copy.21 = bf16[512,3584]{1,0:T(8,128)(2,1)} copy(bf16[512,3584]{0,1:T(8,128)(2,1)} %slice.33) | data formatting | bytes 7340032
  203.7 0.0 copy-start.6
  203.8 123.4 %all-reduce.2.cloned.1.call-done = bf16[512,3584]{1,0:T(8,128)(2,1)} async-done(((bf16[512,3584]{1,0:T(8,128)(2,1)}), bf16[512,3584]{1,0:T(8,128)(2,1)}) %all-reduce.2.cloned.1.call-update) | async-done | bytes 3670032 | tf_op jit(solution)/shard_map/psum | solution.py:100
  327.2 0.0 copy-start.4
  327.2 4.9 %fusion.16 = (f32[512]{0:T(512)S(1)}, bf16[512,3584]{1,0:T(8,128)(2,1)S(1)}) fusion(bf16[512,3584]{1,0:T(8,128)(2,1)} %all-reduce.2.cloned.1.call-done, bf16[512,3584]{1,0:T(8,128)(2,1)} %copy.21), kind=kLoop, calls=%fused_computation.25 | loop fusion | flops 12844544 | bytes 11012096 | tf_op jit(solution)/shard_map/reduce_sum | solution.py:12
  332.1 0.0 copy-start.2
  332.1 1.8 copy-done.2
  333.9 0.0 copy-done.6
  333.9 0.0 copy-done.4
  333.9 3.1 fusion.40
  337.0 0.0 copy-done
  337.0 9.0 %convolution_convert_fusion.1 = bf16[512,3584]{1,0:T(8,128)(2,1)} fusion(bf16[448,3584]{1,0:T(8,128)(2,1)S(1)} %copy-done, f32[512,448]{0,1:T(8,128)} %fusion.40, bf16[3584,448]{0,1:T(8,128)(2,1)} %param.22, bf16[512,3584]{1,0:T(8,128)(2,1)} %copy-done.2, f32[3584]{0:T(1024)S(1)} %copy-done.6, f32[512]{0:T(512)S(1)} %add_rsqrt_fusion), kind=kOutput, calls=%fused_computation.33 | convolution fusion | flops 3297968128 | bytes 14696448 | tf_op jit(solution)/shard_map/dot_general | solution.py:110
  346.0 0.0 reduce-scatter.2.cloned.1.call-update
  346.0 81.3 %reduce-scatter.2.cloned.1.call-done = bf16[16,3584]{1,0:T(8,128)(2,1)} async-done(((bf16[512,3584]{1,0:T(8,128)(2,1)}), bf16[16,3584]{1,0:T(8,128)(2,1)}) %reduce-scatter.2.cloned.1.call-update) | async-done | bytes 114704 | tf_op jit(solution)/shard_map/reduce_scatter | solution.py:109
  427.4 1.6 add_convert_fusion.1
  (17 shorter events, 0.1 us)
Async XLA Ops:
  6.5 330.5 %copy-start = (bf16[448,3584]{1,0:T(8,128)(2,1)S(1)}, bf16[448,3584]{1,0:T(8,128)(2,1)}, u32[]{:S(2)}) copy-start(bf16[448,3584]{1,0:T(8,128)(2,1)} %param.23) | copy-start | bytes 9633796
  6.5 56.5 %all-gather.3.cloned.1.call-start = ((), (), s32[]{:S(2)}) async-start(), calls=%async_computation.1 | async-start | bytes 7569408 | tf_op jit(solution)/shard_map/all_gather | solution.py:57
  7.3 150.0 %all-gather.5.cloned.1.call-start = ((), (), s32[]{:S(2)}) async-start(), calls=%async_computation.2 | async-start | bytes 12042240 | tf_op jit(solution)/shard_map/all_gather | solution.py:62
  8.0 319.2 %all-reduce.2.cloned.1.call-start = ((), (), s32[]{:S(2)}) async-start(), calls=%async_computation.3 | async-start | bytes 7340032 | tf_op jit(solution)/shard_map/psum | solution.py:100
  8.7 148.6 %copy-start.5 = (f32[7168]{0:T(1024)S(1)}, f32[7168]{0:T(1024)}, u32[]{:S(2)}) copy-start(f32[7168]{0:T(1024)} %param.14) | copy-start | bytes 86020
  168.3 1.8 copy-start.3
  186.9 1.0 copy-start.1
  193.5 233.9 %reduce-scatter.2.cloned.1.call-start = ((), (), s32[]{:S(2)}) async-start(), calls=%async_computation.4 | async-start | bytes 3784704 | tf_op jit(solution)/shard_map/reduce_scatter | solution.py:109
  203.7 130.1 %copy-start.6 = (f32[3584]{0:T(1024)S(1)}, f32[3584]{0:T(1024)}, u32[]{:S(2)}) copy-start(f32[3584]{0:T(1024)} %param.20) | copy-start | bytes 43012
  327.2 6.7 %copy-start.4 = (bf16[3584,448]{0,1:T(8,128)(2,1)S(1)}, bf16[3584,448]{0,1:T(8,128)(2,1)}, u32[]{:S(2)}) copy-start(bf16[3584,448]{0,1:T(8,128)(2,1)} %param.21) | copy-start | bytes 9633796
  332.1 1.8 copy-start.2
Sparse Core Ops, SparseCore 0:
  9.6 53.3 all-gather.2
  64.7 92.5 all-gather.4
  193.6 133.5 all-reduce.1
  346.1 81.1 reduce-scatter.1
where the time goes:
time: 436 us
  waiting for transfers between devices  350 us (80%)
  matrix products  41 us (9%)
  other arithmetic  16.4 us (4%)
  between operations  13.9 us (3%)
  local copies, waits for them, and re-layouts  13.8 us (3%)
    psum x1, waiting for transfers between devices, shards(): lax.psum(jnp.dot(heads_out, out_weight, preferred_element_type=jnp.float3...  123 us
    all_gather x1, waiting for transfers between devices, shards(): lax.all_gather(qkv_weight, 'req', axis=0, tiled=True)  89.6 us
    reduce_scatter x1, waiting for transfers between devices, shards(): lax.psum_scatter(jnp.dot(hidden, down_weight, preferred_element_type=jnp....  81.3 us
    all_gather x1, waiting for transfers between devices, shards(): whole_input = lax.all_gather(layer_input, 'hid', axis=1, tiled=True)  54.3 us
    dot_general x1, matrix products, shards(): jnp.dot(columns, lax.all_gather(qkv_weight, 'req', axis=0, tiled=True), p...  11 us
    reduce_sum x2, other arithmetic, rms_scale(): jnp.mean(values * values, axis=-1, keepdims=True) + epsilon  9.55 us
    dot_general x1, matrix products, shards(): jnp.dot(hidden, down_weight, preferred_element_type=jnp.float32)  8.99 us
    unnamed x15, local copies, waits for them, and re-layouts  8.73 us
  transfers between devices with their start and end apart: 4, of which 4 were waited for; matrix products, arithmetic and copies ran while one was open for 3% of the time, Pallas kernels for 0%

commit v1 on v0

--- a/solution.py
+++ b/solution.py
@@ -54,7 +54,9 @@
     heads_dev = cache_keys.shape[2] // HD
     slots = cache_keys.shape[1]
     scale = HD ** (-0.5)
-    whole_input = lax.all_gather(layer_input, "hid", axis=1, tiled=True)
+    whole_input = jnp.concatenate(
+        lax.all_to_all(jnp.stack([layer_input] * lax.axis_size("hid")), "hid", 0, 0), axis=1
+    )
     normed = rms_scale(whole_input.astype(jnp.float32), norm_gain).astype(jnp.bfloat16)
     columns = normed
     projected = jnp.dot(

time: 436 us -> 418 us (0.959)
  waiting for transfers between devices: 350 us -> 312 us
  starting transfers between devices: 0.3 us -> 8.96 us
  other arithmetic: 16.4 us -> 24 us
  local copies, waits for them, and re-layouts: 13.8 us -> 18.8 us
    all_to_all x0 -> x1, waiting for transfers between devices: none -> 97.5 us  [shards(): lax.all_to_all(jnp.stack([layer_input] * lax.axis_size('hid')), 'hid', 0, 0)]
    all_gather x1, waiting for transfers between devices: 89.6 us -> 0.01 us  [shards(): lax.all_gather(qkv_weight, 'req', axis=0, tiled=True)]
    all_gather x1 -> x0, waiting for transfers between devices: 54.3 us -> none  [shards(): whole_input = lax.all_gather(layer_input, 'hid', axis=1, tiled=True)]
    psum x1, waiting for transfers between devices: 123 us -> 132 us  [shards(): lax.psum(jnp.dot(heads_out, out_weight, preferred_element_type=jnp.float3...]
    all_to_all x0 -> x1, starting transfers between devices: none -> 8.69 us  [shards(): lax.all_to_all(jnp.stack([layer_input] * lax.axis_size('hid')), 'hid', 0, 0)]
    convert_element_type x0 -> x1, other arithmetic: none -> 7.15 us  [shards(): rms_scale(whole_input.astype(jnp.float32), norm_gain).astype(jnp.bfloat16)]
    another operation x0 -> x1, local copies, waits for them, and re-layouts: none -> 4.95 us  [shards(): jnp.stack([layer_input] * lax.axis_size('hid'))]
  transfers between devices with their start and end apart: 4 -> 4, of which waited for: 4 -> 3; matrix products, arithmetic and copies ran while one was open for 3% -> 7% of each run, Pallas kernels for 0% -> 0%
where the time goes in v1:
time: 418 us; the launch traced here: 417 us
  waiting for transfers between devices  312 us (75%)
  matrix products  39.7 us (9%)
  other arithmetic  24 us (6%)
  local copies, waits for them, and re-layouts  18.8 us (4%)
  between operations  13.9 us (3%)
  starting transfers between devices  8.96 us (2%)
    psum x1, waiting for transfers between devices, shards(): lax.psum(jnp.dot(heads_out, out_weight, preferred_element_type=jnp.float3...  132 us
    all_to_all x1, waiting for transfers between devices, shards(): lax.all_to_all(jnp.stack([layer_input] * lax.axis_size('hid')), 'hid', 0, 0)  97.5 us
    reduce_scatter x1, waiting for transfers between devices, shards(): lax.psum_scatter(jnp.dot(hidden, down_weight, preferred_element_type=jnp....  81.4 us
    reduce_sum x2, other arithmetic, rms_scale(): jnp.mean(values * values, axis=-1, keepdims=True) + epsilon  9.93 us
    dot_general x1, matrix products, shards(): jnp.dot(columns, lax.all_gather(qkv_weight, 'req', axis=0, tiled=True), p...  9.86 us
    dot_general x1, matrix products, shards(): jnp.dot(hidden, down_weight, preferred_element_type=jnp.float32)  8.99 us
    unnamed x15, local copies, waits for them, and re-layouts  8.76 us
    all_to_all x1, starting transfers between devices, shards(): lax.all_to_all(jnp.stack([layer_input] * lax.axis_size('hid')), 'hid', 0, 0)  8.69 us
  transfers between devices with their start and end apart: 4, of which 3 were waited for; matrix products, arithmetic and copies ran while one was open for 7% of the time, Pallas kernels for 0%

profile of v1, /device:TPU:0, one launch (start us, length us, event | category | flops | bytes accessed | tf_op | source)
XLA Modules:
  0.0 417.1 jit_solution(17828438280275467870)
XLA Ops:
  6.5 0.0 copy-start
  6.5 0.0 all-gather.2.cloned.1.call-start
  6.5 0.7 all-gather.2.cloned.1.call-update
  7.3 4.9 %stack.2 = bf16[32,512,224]{1,2,0:T(8,128)(2,1)} broadcast(bf16[512,224]{0,1:T(8,128)(2,1)} %param.13), dimensions={1,2} | broadcast | bytes 7569408 | tf_op jit(solution)/shard_map/stack | solution.py:58
  12.2 0.0 copy-start.4
  12.2 8.7 %all-to-all-start = ((bf16[32,512,224]{1,2,0:T(8,128)(2,1)}), bf16[32,512,224]{1,2,0:T(8,128)(2,1)}, u32[]{:S(2)}, u32[]{:S(2)}) async-start(bf16[32,512,224]{1,2,0:T(8,128)(2,1)} %stack.2), calls=%async_computation | async-start | bytes 14680064 | tf_op jit(solution)/shard_map/all_to_all | solution.py:58
  20.9 0.0 all-reduce.2.cloned.1.call-start
  21.6 0.0 copy-done.4
  21.6 0.1 mul.172
  21.7 97.5 %all-to-all-done = bf16[32,512,224]{1,2,0:T(8,128)(2,1)} async-done(((bf16[32,512,224]{1,2,0:T(8,128)(2,1)}), bf16[32,512,224]{1,2,0:T(8,128)(2,1)}, u32[]{:S(2)}, u32[]{:S(2)}) %all-to-all-start) | async-done | bytes 7340064 | tf_op jit(solution)/shard_map/all_to_all | solution.py:58
  119.2 5.0 %fusion.13 = f32[512]{0:T(512)S(1)} fusion(bf16[32,512,224]{1,2,0:T(8,128)(2,1)} %all-to-all-done), kind=kLoop, calls=%fused_computation.20 | loop fusion | flops 11009536 | bytes 7342080 | tf_op jit(solution)/shard_map/reduce_sum | solution.py:12
  124.2 7.1 %fusion.15 = bf16[512,32,224]{0,2,1:T(8,128)(2,1)} fusion(bf16[32,512,224]{1,2,0:T(8,128)(2,1)} %all-to-all-done, f32[32,224]{1,0:T(8,128)S(1)} %mul.172, f32[512]{0:T(512)S(1)} %add_rsqrt_fusion.1), kind=kLoop, calls=%fused_computation.22 | loop fusion | flops 14680064 | bytes 14710784 | tf_op jit(solution)/shard_map/convert_element_type | solution.py:60
  131.4 0.0 all-gather.2.cloned.1.call-done
  131.4 9.9 %convolution_bitcast_fusion.1 = f32[512,1,3,224]{0,3,2,1:T(8,128)S(1)} fusion(bf16[512,7168,1]{0,1,2:T(8,128)(2,1)} %bitcast.100, bf16[3,224,7168]{2,1,0:T(8,128)(2,1)} %bitcast.115), kind=kOutput, calls=%fused_computation.31 | convolution fusion | flops 4932501504 | bytes 18350080 | tf_op jit(solution)/shard_map/dot_general | solution.py:62
  141.3 0.0 copy-start.3
  141.3 0.1 slice_bitcast_fusion
  141.3 1.7 fusion.74
  143.0 0.0 copy-done.3
  143.0 0.7 pad_maximum_fusion
  143.8 0.8 broadcast_in_dim.26
  144.6 13.8 %while.14 = (s32[]{:T(128)}, f32[1,512]{1,0:T(1,128)S(1)}, f32[1,512]{1,0:T(1,128)S(1)}, f32[512,1,224]{0,2,1:T(8,128)}, s32[]{:T(128)}, /*index=5*/s32[]{:T(128...) while((s32[]{:T(128)}, f32[1,512]{1,0:T(1,128)S(1)}, ...), condition=%wide.region_4.5_spmd, body=%wide.region_1.4_spmd.sunk | while | flops 236947456 | bytes 4785347 | solution.py:90
  144.6 0.7 add_compare_fusion.2
  145.3 1.4 fusion.91
  146.7 0.2 fusion.92
  146.9 2.3 fusion.93
  149.2 0.7 add_compare_fusion.2
  149.9 1.4 fusion.91
  151.3 0.2 fusion.92
  151.5 2.3 fusion.93
  153.8 0.7 add_compare_fusion.2
  154.5 1.4 fusion.91
  155.9 0.2 fusion.92
  156.1 2.3 fusion.93
  158.4 1.3 fusion.77
  159.7 0.0 copy-start.1
  159.7 1.0 copy-done.1
  160.7 0.2 fusion.28
  160.9 5.3 %convolution_convert_fusion = bf16[512,3584]{1,0:T(8,128)(2,1)} fusion(bf16[224,3584]{1,0:T(8,128)(2,1)} %param.19, f32[512,512]{0,1:T(8,128)} %copy-done.1, f32[512]{0:T(512)S(1)} %bitcast.110, f32[512,1,224]{0,2,1:T(8,128)} %get-tuple-element.55, f32[512,1,3,224]{0,3,2,1:T(8,128)} %copy-done.3, f32[512]{0:T(512)S(1)} %bitcast.112, f32[512]{0:T(512)S(1)} %bitcast.113), kind=kOutput, calls=%fused_computation.29 | convolution fusion | flops 942342144 | bytes 7018496 | tf_op jit(solution)/shard_map/dot_general | solution.py:103
  166.2 0.0 all-reduce.2.cloned.1.call-update
  166.2 0.2 reduce-scatter.2.cloned.1.call-start
  166.5 4.1 slice.33
  170.5 6.0 %copy.20 = bf16[512,3584]{1,0:T(8,128)(2,1)} copy(bf16[512,3584]{0,1:T(8,128)(2,1)} %slice.33) | data formatting | bytes 7340032
  176.5 0.0 copy-start.6
  176.5 132.2 %all-reduce.2.cloned.1.call-done = bf16[512,3584]{1,0:T(8,128)(2,1)} async-done(((bf16[512,3584]{1,0:T(8,128)(2,1)}), bf16[512,3584]{1,0:T(8,128)(2,1)}) %all-reduce.2.cloned.1.call-update) | async-done | bytes 3670032 | tf_op jit(solution)/shard_map/psum | solution.py:102
  308.8 0.0 copy-start.5
  308.8 4.9 %fusion.16 = (f32[512]{0:T(512)S(1)}, bf16[512,3584]{1,0:T(8,128)(2,1)S(1)}) fusion(bf16[512,3584]{1,0:T(8,128)(2,1)} %all-reduce.2.cloned.1.call-done, bf16[512,3584]{1,0:T(8,128)(2,1)} %copy.20), kind=kLoop, calls=%fused_computation.25 | loop fusion | flops 12844544 | bytes 11012096 | tf_op jit(solution)/shard_map/reduce_sum | solution.py:12
  313.7 0.0 copy-start.2
  313.7 1.8 copy-done.2
  315.5 0.0 copy-done.6
  315.5 0.0 copy-done.5
  315.5 3.1 fusion.36
  318.6 0.0 copy-done
  318.6 9.0 %convolution_convert_fusion.1 = bf16[512,3584]{1,0:T(8,128)(2,1)} fusion(bf16[448,3584]{1,0:T(8,128)(2,1)S(1)} %copy-done, f32[512,448]{0,1:T(8,128)} %fusion.36, bf16[3584,448]{0,1:T(8,128)(2,1)} %param.22, bf16[512,3584]{1,0:T(8,128)(2,1)} %copy-done.2, f32[3584]{0:T(1024)S(1)} %copy-done.6, f32[512]{0:T(512)S(1)} %add_rsqrt_fusion), kind=kOutput, calls=%fused_computation.30 | convolution fusion | flops 3297968128 | bytes 14696448 | tf_op jit(solution)/shard_map/dot_general | solution.py:112
  327.6 0.0 reduce-scatter.2.cloned.1.call-update
  327.6 81.4 %reduce-scatter.2.cloned.1.call-done = bf16[16,3584]{1,0:T(8,128)(2,1)} async-done(((bf16[512,3584]{1,0:T(8,128)(2,1)}), bf16[16,3584]{1,0:T(8,128)(2,1)}) %reduce-scatter.2.cloned.1.call-update) | async-done | bytes 114704 | tf_op jit(solution)/shard_map/reduce_scatter | solution.py:111
  409.0 1.6 add_convert_fusion.1
  (17 shorter events, 0.1 us)
Async XLA Ops:
  6.5 312.1 %copy-start = (bf16[448,3584]{1,0:T(8,128)(2,1)S(1)}, bf16[448,3584]{1,0:T(8,128)(2,1)}, u32[]{:S(2)}) copy-start(bf16[448,3584]{1,0:T(8,128)(2,1)} %param.23) | copy-start | bytes 9633796
  6.5 124.9 %all-gather.2.cloned.1.call-start = ((), (), s32[]{:S(2)}) async-start(), calls=%async_computation.2 | async-start | bytes 12042240 | tf_op jit(solution)/shard_map/all_gather | solution.py:64
  12.2 9.4 %copy-start.4 = (f32[7168]{0:T(1024)S(1)}, f32[7168]{0:T(1024)}, u32[]{:S(2)}) copy-start(f32[7168]{0:T(1024)} %param.14) | copy-start | bytes 86020
  12.2 107.0 %all-to-all-start = ((bf16[32,512,224]{1,2,0:T(8,128)(2,1)}), bf16[32,512,224]{1,2,0:T(8,128)(2,1)}, u32[]{:S(2)}, u32[]{:S(2)}) async-start(bf16[32,512,224]{1,2,0:T(8,128)(2,1)} %stack.2), calls=%async_computation | async-start | bytes 14680064 | tf_op jit(solution)/shard_map/all_to_all | solution.py:58
  20.9 287.9 %all-reduce.2.cloned.1.call-start = ((), (), s32[]{:S(2)}) async-start(), calls=%async_computation.3 | async-start | bytes 7340032 | tf_op jit(solution)/shard_map/psum | solution.py:102
  141.3 1.8 copy-start.3
  159.7 1.0 copy-start.1
  166.2 242.7 %reduce-scatter.2.cloned.1.call-start = ((), (), s32[]{:S(2)}) async-start(), calls=%async_computation.4 | async-start | bytes 3784704 | tf_op jit(solution)/shard_map/reduce_scatter | solution.py:111
  176.5 138.9 %copy-start.6 = (f32[3584]{0:T(1024)S(1)}, f32[3584]{0:T(1024)}, u32[]{:S(2)}) copy-start(f32[3584]{0:T(1024)} %param.20) | copy-start | bytes 43012
  308.8 6.7 %copy-start.5 = (bf16[3584,448]{0,1:T(8,128)(2,1)S(1)}, bf16[3584,448]{0,1:T(8,128)(2,1)}, u32[]{:S(2)}) copy-start(bf16[3584,448]{0,1:T(8,128)(2,1)} %param.21) | copy-start | bytes 9633796
  313.7 1.8 copy-start.2
Sparse Core Ops, SparseCore 0:
  9.0 96.0 all-gather.1
  166.3 142.3 all-reduce.1
  327.7 81.1 reduce-scatter.1
